TPU v7x, 512 devices: a whole 4x8x8 slice. The times are simulated.
512 devices in a mesh: wide: 32 (over z_lo, x, core), narrow: 16 (over z_hi, y).
Axes of the slice: x: 4, y: 8, z: 8 (z_hi: 2, z_lo: 4; z = z_hi * 4 + z_lo), core: 2. Of those that a mesh axis runs over, the one named last changes fastest.
Arguments:
- exposures: bfloat16 [4, 512, 12288], P(None, 'narrow', 'wide'), may hold values from -6 to 6
- basis_kernels: bfloat16 [5, 21, 21], replicated, may hold values from -0.25 to 0.25
- poly_coef: float32 [4, 5, 6], replicated, may hold values from -3 to 3
- exposure_weight: float32 [4], replicated, may hold values from 0.5 to 2
- row_start: int32 [4], replicated, may hold values from 0 to 256, as said below
- row_count: int32 [4], replicated, may hold values from 128 to 512, as said below
- filter_taps: float32 [21], replicated, may hold values from -1.5 to 1.5
Outputs:
- coadded: float32 [512, 12288], P('narrow', 'wide')
- detection: float32 [512, 12288], P('narrow', 'wide')
Inputs may be any that keep to these rules, and one draw needn't show every extreme that they name: Each row_start is a multiple of 32; row_start[0] is 0 and row_start + row_count never exceeds 512. Each row_count is a multiple of 8; exposure 0 covers the whole band.
All inputs are finite; a program needn't handle non-finite values.
Results may differ from a plain program's by a relative error of at most 0.0003.
Values may be sent and summed in bfloat16 or wider, within the bound.
A program may use at most 64 MiB of HBM per device.

v0:
```python
import math
import jax
import jax.numpy as jnp
from jax import lax
from jax.sharding import PartitionSpec as P


def padded(array, sides, width):
    for axis, dim in sides:
        peers, length = (lax.axis_size(axis), array.shape[dim])
        up = [(i, (i + 1) % peers) for i in range(peers - 1)]
        down = [(j, i) for i, j in up]
        last = lax.slice_in_dim(array, length - width, length, axis=dim)
        initial = lax.slice_in_dim(array, 0, width, axis=dim)
        before = lax.ppermute(last, axis, up)
        after = lax.ppermute(initial, axis, down)
        array = jnp.concatenate([before, array, after], axis=dim)
    return array


def respond(window, basis_kernels):
    side = basis_kernels.shape[1]
    kernel_total = basis_kernels.shape[0]
    out_rows = window.shape[0] - (side - 1)
    out_cols = window.shape[1] - (side - 1)
    block = math.gcd(out_cols, 128)
    block_total = out_cols // block
    span = block + side - 1
    shifted = jnp.stack([window[offset : offset + out_rows] for offset in range(side)])
    patches = jnp.stack(
        [shifted[:, :, index * block : index * block + span] for index in range(block_total)]
    )
    lagged = (
        jnp.arange(span, dtype=jnp.int32)[:, None] - jnp.arange(block, dtype=jnp.int32)[None, :]
    )
    onehot = (lagged[None] == jnp.arange(side, dtype=jnp.int32)[:, None, None]).astype(jnp.float32)
    table = jnp.einsum(
        "kab,bco->acko", basis_kernels.astype(jnp.float32), onehot, precision=lax.Precision.HIGHEST
    )
    table = table.astype(jnp.bfloat16).reshape(side, span, kernel_total * block)
    result = jnp.einsum("jarc,acn->jrn", patches, table, preferred_element_type=jnp.float32)
    result = result.reshape(block_total, out_rows, kernel_total, block).transpose(2, 1, 0, 3)
    return result.reshape(kernel_total, out_rows, out_cols)


def on_device(
    exposures, basis_kernels, poly_coef, exposure_weight, row_start, row_count, filter_taps
):
    tile_rows = exposures.shape[1]
    tile_cols = exposures.shape[2]
    band_rows = tile_rows * lax.axis_size("narrow")
    band_cols = tile_cols * lax.axis_size("wide")
    row_base = lax.axis_index("narrow") * tile_rows
    row_index = row_base + jnp.arange(tile_rows, dtype=jnp.int32)
    col_index = lax.axis_index("wide") * tile_cols + jnp.arange(tile_cols, dtype=jnp.int32)
    y_coord = ((2 * row_index + 1).astype(jnp.float32) / band_rows - 1.0)[:, None]
    x_coord = ((2 * col_index + 1).astype(jnp.float32) / band_cols - 1.0)[None, :]
    numerator = jnp.zeros((tile_rows, tile_cols), jnp.float32)
    denominator = jnp.zeros((tile_rows, 1), jnp.float32)
    zero_value = jnp.zeros((), exposures.dtype)
    for member in range(exposures.shape[0]):
        first_row = row_start[member]
        row_total = row_count[member]
        inside = (row_index >= first_row) & (row_index < first_row + row_total)
        lead_row = row_base - 10 - first_row

        def placed_rows(window, portion, anchor, lead_row=lead_row):
            window_len = window.shape[0]
            portion_len = portion.shape[0]
            padding = jnp.zeros((window_len, portion.shape[1]), portion.dtype)
            extended = jnp.concatenate([padding, portion, padding], 0)
            sliced = lax.dynamic_slice_in_dim(extended, lead_row + window_len, window_len, 0)
            local_rows = lead_row + jnp.arange(window_len, dtype=jnp.int32)
            present = (local_rows >= 0) & (local_rows < portion_len)
            return jnp.where(present[:, None], sliced, window)

        empty_window = jnp.zeros((tile_rows + 20, tile_cols), exposures.dtype)
        window = placed_rows(
            empty_window,
            lax.all_gather(exposures[member], "narrow", axis=0, tiled=True),
            jnp.int32(0),
        )
        window_rows = row_base - 10 + jnp.arange(tile_rows + 20, dtype=jnp.int32)
        valid_rows = (window_rows >= first_row) & (window_rows < first_row + row_total)
        window = jnp.where(valid_rows[:, None], window, zero_value)
        window = padded(window, (("wide", 1),), 10)
        touches = (first_row < row_base + tile_rows) & (first_row + row_total > row_base)

        def matched_tile(window, member=member):
            response = respond(window, basis_kernels)
            matched = jnp.zeros((tile_rows, tile_cols), jnp.float32)
            for kernel in range(basis_kernels.shape[0]):
                coeffs = poly_coef[member, kernel]
                spatial = (
                    coeffs[0]
                    + coeffs[1] * x_coord
                    + coeffs[2] * y_coord
                    + coeffs[3] * x_coord * x_coord
                    + coeffs[4] * x_coord * y_coord
                    + coeffs[5] * y_coord * y_coord
                )
                matched = matched + spatial * response[kernel]
            return matched

        def empty_tile(window):
            return jnp.zeros((tile_rows, tile_cols), jnp.float32)

        matched = lax.cond(touches, matched_tile, empty_tile, window)
        weighting = exposure_weight[member] * inside.astype(jnp.float32)[:, None]
        numerator = numerator + weighting * matched
        denominator = denominator + weighting
    coadded = numerator / denominator
    taps_total = filter_taps.shape[0]
    framed = padded(coadded, (("wide", 1),), 10)
    inner = filter_taps[0] * framed[:, 0:tile_cols]
    for offset in range(1, taps_total):
        inner = inner + filter_taps[offset] * framed[:, offset : offset + tile_cols]
    across = padded(inner, (("narrow", 0),), 10)
    detection = filter_taps[0] * across[0:tile_rows]
    for offset in range(1, taps_total):
        detection = detection + filter_taps[offset] * across[offset : offset + tile_rows]
    return (coadded, detection)


def solution(mesh):
    placed = (P(None, "narrow", "wide"), P(), P(), P(), P(), P(), P())
    return jax.shard_map(
        on_device,
        mesh=mesh,
        in_specs=placed,
        out_specs=(P("narrow", "wide"), P("narrow", "wide")),
        check_vma=False,
    )
```

profile of v0, /device:TPU:384, one launch (start us, length us, event | category | flops | bytes accessed | tf_op | source)
XLA Modules:
  0.0 495.4 jit_solution(2599510035167982765)
XLA Ops:
  0.7 1.5 fusion.263
  2.2 1.4 fusion.262
  5.6 0.8 fusion.252
  6.4 50.4 %all-gather.3 = bf16[1,512,384]{2,1,0:T(8,128)(2,1)S(1)} all-gather(bf16[1,32,384]{2,1,0:T(8,128)(2,1)S(1)} %get-tuple-element.333), channel_id=5, replica_groups=mesh['wide'=32,'narrow'=16] {'narrow'}, dimensions={1}, use_global_device_ids=true | all-gather | bytes 417792 | tf_op jit(solution)/shard_map/all_gather | solution.py:80
  57.7 1.9 collective-permute-start.7
  59.7 2.4 collective-permute-start.6
  65.1 50.3 %all-gather = bf16[1,512,384]{2,1,0:T(8,128)(2,1)S(1)} all-gather(bf16[1,32,384]{2,1,0:T(8,128)(2,1)S(1)} %get-tuple-element.331), channel_id=2, replica_groups=mesh['wide'=32,'narrow'=16] {'narrow'}, dimensions={1}, use_global_device_ids=true | all-gather | bytes 417792 | tf_op jit(solution)/shard_map/all_gather | solution.py:80
  117.3 49.7 %all-gather.1 = bf16[1,512,384]{2,1,0:T(8,128)(2,1)S(1)} all-gather(bf16[1,32,384]{2,1,0:T(8,128)(2,1)S(1)} %get-tuple-element.332), channel_id=3, replica_groups=mesh['wide'=32,'narrow'=16] {'narrow'}, dimensions={1}, use_global_device_ids=true | all-gather | bytes 417792 | tf_op jit(solution)/shard_map/all_gather | solution.py:80
  168.3 49.0 %all-gather.2 = bf16[1,512,384]{2,1,0:T(8,128)(2,1)S(1)} all-gather(bf16[1,32,384]{2,1,0:T(8,128)(2,1)S(1)} %get-tuple-element.334), channel_id=4, replica_groups=mesh['wide'=32,'narrow'=16] {'narrow'}, dimensions={1}, use_global_device_ids=true | all-gather | bytes 417792 | tf_op jit(solution)/shard_map/all_gather | solution.py:80
  217.3 1.2 compare_and_fusion.3
  219.0 1.9 collective-permute-start.5
  220.9 2.4 collective-permute-start.4
  223.4 5.3 %collective-permute-start.3 = (bf16[52,10]{1,0:T(8,128)(2,1)S(1)}, bf16[52,10]{1,0:T(8,128)(2,1)S(1)}, u32[]{:S(2)}, u32[]{:S(2)}) collective-permute-start(bf16[52,10]{1,0:T(8,128)(2,1)S(1)} %get-tuple-element.345), channel_id=1, source_target_pairs={{16,0},{32,16},{48,32},{64,48},{80,64},{96,80},{112,96},{128,112},... | collective-permute-start | bytes 3128 | tf_op jit(solution)/shard_map/ppermute | solution.py:16
  230.1 5.0 %add_add_fusion = (f32[32]{0:T(128)S(1)}, f32[32]{0:T(128)S(1)}, f32[32]{0:T(128)S(1)}, f32[32]{0:T(128)S(1)}, f32[32]{0:T(128)S(1)}) fusion(f32[]{:T(128)} %bitcast.314, s32[]{:T(128)S(6)} %add.1350, s32[]{:T(128)} %bitcast.312, s32[]{:T(128)S(6)} %mul.1366, f32[]{:T(128)} %bitcast.310, s32[]{:T(128)S(6)} %add.1334, s32[]{:T(128)} %bitcast.308, ...), kind=kLoop, calls=%fused_computation.570 | loop fusion | flops 640 | bytes 692 | tf_op jit(solution)/shard_map/add | solution.py:111
  237.8 1.9 collective-permute-start.2
  239.7 5.8 %collective-permute-start.1 = (bf16[52,10]{1,0:T(8,128)(2,1)S(1)}, bf16[52,10]{1,0:T(8,128)(2,1)S(1)}, u32[]{:S(2)}, u32[]{:S(2)}) collective-permute-start(bf16[52,10]{1,0:T(8,128)(2,1)S(1)} %get-tuple-element.340), channel_id=1, source_target_pairs={{16,0},{32,16},{48,32},{64,48},{80,64},{96,80},{112,96},{128,112},... | collective-permute-start | bytes 3128 | tf_op jit(solution)/shard_map/ppermute | solution.py:16
  245.6 1.9 collective-permute-start
  247.7 5.0 %collective-permute-done = bf16[52,10]{1,0:T(8,128)(2,1)S(1)} collective-permute-done((bf16[52,10]{1,0:T(8,128)(2,1)S(1)}, bf16[52,10]{1,0:T(8,128)(2,1)S(1)}, u32[]{:S(2)}, u32[]{:S(2)}) %collective-permute-start) | collective-permute-done | bytes 1072 | tf_op jit(solution)/shard_map/ppermute | solution.py:15
  252.8 48.0 %conditional.7 = (f32[32,384]{1,0:T(8,128)S(1)}) conditional(s32[]{:T(128)} %convert_element_type.81, () %tuple.38, (f32[4,5,6]{2,0,1:T(4,128)S(1)}, f32[1,384]{1,0:T(1,128)S(1)}, f32[32,1]{0,1:T(1,128)S(1)}, bf16[52,404]{1,0:T(8,128)(2,1)S(1)}, bf16[5,21,21]{2,1,0:T(8,128)(2,1)S(1)}) %tuple.324), branch_computations={%region_6.7_spmd, %region_7.8_spmd} | conditional | flops 470078048 | bytes 36717480 | solution.py:108
  252.9 1.3 convert_bitcast_fusion.3
  254.2 3.9 copy.30
  258.1 8.9 %reshape.485 = bf16[21,148,640]{2,1,0:T(8,128)(2,1)} reshape(bf16[21,148,5,128]{3,2,1,0:T(8,128)(2,1)} %copy.30) | data formatting | bytes 7956480 | tf_op jit(solution)/shard_map/cond/branch_1_fun/reshape | solution.py:40
  267.0 8.8 %dot_general.38 = bf16[5,128,21,148]{1,0,3,2:T(8,128)(2,1)} reshape(bf16[640,21,148]{0,2,1:T(8,128)(2,1)} %bitcast.689) | data formatting | bytes 7956480 | tf_op jit(solution)/shard_map/cond/branch_1_fun/jarc,acn->jrn/dot_general | solution.py:41
  276.3 3.8 fusion.92
  280.4 0.7 fusion.250
  281.8 6.2 %multiply_bitcast_fusion.19 = (f32[32]{0:T(128)S(1)}, f32[32]{0:T(128)S(1)}, f32[32]{0:T(128)S(1)}, f32[32]{0:T(128)S(1)}, f32[32]{0:T(128)S(1)}, /*index=5*/f32...) fusion(f32[32,1]{0,1:T(1,128)S(1)} %get-tuple-element.69, f32[]{:T(128)} %bitcast.233, ...), kind=kLoop, calls=%fused_computation.334 | loop fusion | flops 480 | bytes 1448 | tf_op jit(solution)/shard_map/cond/branch_1_fun/add | solution.py:95
  288.0 11.3 %add_reduce_fusion.19 = (f32[384]{0:T(512)S(1)}, f32[384]{0:T(512)S(1)}, f32[384]{0:T(512)S(1)}, f32[384]{0:T(512)S(1)}, f32[384]{0:T(512)S(1)}, /*index=5*/f32[...) fusion(f32[1,384]{1,0:T(1,128)S(1)} %get-tuple-element.68, ...), kind=kLoop, calls=%fused_computation.319 | loop fusion | flops 8448 | bytes 21576 | tf_op jit(solution)/shard_map/cond/branch_1_fun/add | solution.py:95
  299.3 1.4 fusion.105
  300.8 48.2 %conditional.6 = (f32[32,384]{1,0:T(8,128)S(1)}) conditional(s32[]{:T(128)} %convert_element_type.80, () %tuple.36, (f32[4,5,6]{2,0,1:T(4,128)S(1)}, f32[1,384]{1,0:T(1,128)S(1)}, f32[32,1]{0,1:T(1,128)S(1)}, bf16[52,404]{1,0:T(8,128)(2,1)S(1)}, bf16[5,21,21]{2,1,0:T(8,128)(2,1)S(1)}) %tuple.325), branch_computations={%region_4.5_spmd, %region_5.6_spmd} | conditional | flops 470078048 | bytes 36717480 | solution.py:108
  301.1 1.3 convert_bitcast_fusion.2
  302.4 3.9 copy.23
  306.3 8.9 %reshape.484 = bf16[21,148,640]{2,1,0:T(8,128)(2,1)} reshape(bf16[21,148,5,128]{3,2,1,0:T(8,128)(2,1)} %copy.23) | data formatting | bytes 7956480 | tf_op jit(solution)/shard_map/cond/branch_1_fun/reshape | solution.py:40
  315.2 8.8 %dot_general.34 = bf16[5,128,21,148]{1,0,3,2:T(8,128)(2,1)} reshape(bf16[640,21,148]{0,2,1:T(8,128)(2,1)} %bitcast.690) | data formatting | bytes 7956480 | tf_op jit(solution)/shard_map/cond/branch_1_fun/jarc,acn->jrn/dot_general | solution.py:41
  324.5 3.8 fusion.63
  328.6 0.7 fusion.247
  330.0 6.3 %multiply_bitcast_fusion.14 = (f32[32]{0:T(128)S(1)}, f32[32]{0:T(128)S(1)}, f32[32]{0:T(128)S(1)}, f32[32]{0:T(128)S(1)}, f32[32]{0:T(128)S(1)}, /*index=5*/f32...) fusion(f32[32,1]{0,1:T(1,128)S(1)} %get-tuple-element.64, f32[]{:T(128)} %bitcast.156, ...), kind=kLoop, calls=%fused_computation.250 | loop fusion | flops 480 | bytes 1448 | tf_op jit(solution)/shard_map/cond/branch_1_fun/add | solution.py:95
  336.3 11.3 %add_reduce_fusion.14 = (f32[384]{0:T(512)S(1)}, f32[384]{0:T(512)S(1)}, f32[384]{0:T(512)S(1)}, f32[384]{0:T(512)S(1)}, f32[384]{0:T(512)S(1)}, /*index=5*/f32[...) fusion(f32[1,384]{1,0:T(1,128)S(1)} %get-tuple-element.63, ...), kind=kLoop, calls=%fused_computation.235 | loop fusion | flops 8448 | bytes 21576 | tf_op jit(solution)/shard_map/cond/branch_1_fun/add | solution.py:95
  347.6 1.3 fusion.76
  349.0 48.2 %conditional.5 = (f32[32,384]{1,0:T(8,128)S(1)}) conditional(s32[]{:T(128)} %convert_element_type.79, () %tuple.34, (f32[4,5,6]{2,0,1:T(4,128)S(1)}, f32[1,384]{1,0:T(1,128)S(1)}, f32[32,1]{0,1:T(1,128)S(1)}, bf16[52,404]{1,0:T(8,128)(2,1)S(1)}, bf16[5,21,21]{2,1,0:T(8,128)(2,1)S(1)}) %tuple.326), branch_computations={%region_2.3_spmd, %region_3.4_spmd} | conditional | flops 470078048 | bytes 36717480 | solution.py:108
  349.3 1.3 convert_bitcast_fusion.1
  350.6 3.9 copy.16
  354.5 8.9 %reshape.483 = bf16[21,148,640]{2,1,0:T(8,128)(2,1)} reshape(bf16[21,148,5,128]{3,2,1,0:T(8,128)(2,1)} %copy.16) | data formatting | bytes 7956480 | tf_op jit(solution)/shard_map/cond/branch_1_fun/reshape | solution.py:40
  363.4 8.8 %dot_general.26 = bf16[5,128,21,148]{1,0,3,2:T(8,128)(2,1)} reshape(bf16[640,21,148]{0,2,1:T(8,128)(2,1)} %bitcast.691) | data formatting | bytes 7956480 | tf_op jit(solution)/shard_map/cond/branch_1_fun/jarc,acn->jrn/dot_general | solution.py:41
  372.7 3.8 fusion.34
  378.2 6.2 %multiply_bitcast_fusion.9 = (f32[32]{0:T(128)S(1)}, f32[32]{0:T(128)S(1)}, f32[32]{0:T(128)S(1)}, f32[32]{0:T(128)S(1)}, f32[32]{0:T(128)S(1)}, /*index=5*/f32[...) fusion(f32[32,1]{0,1:T(1,128)S(1)} %get-tuple-element.59, f32[]{:T(128)} %bitcast.79, ...), kind=kLoop, calls=%fused_computation.166 | loop fusion | flops 480 | bytes 1448 | tf_op jit(solution)/shard_map/cond/branch_1_fun/add | solution.py:95
  384.5 11.2 %add_reduce_fusion.9 = (f32[384]{0:T(512)S(1)}, f32[384]{0:T(512)S(1)}, f32[384]{0:T(512)S(1)}, f32[384]{0:T(512)S(1)}, f32[384]{0:T(512)S(1)}, /*index=5*/f32[3...) fusion(f32[1,384]{1,0:T(1,128)S(1)} %get-tuple-element.58, ...), kind=kLoop, calls=%fused_computation.151 | loop fusion | flops 8448 | bytes 21576 | tf_op jit(solution)/shard_map/cond/branch_1_fun/add | solution.py:95
  395.7 1.3 fusion.47
  397.2 48.2 %conditional.4 = (f32[32,384]{1,0:T(8,128)S(1)}) conditional(s32[]{:T(128)} %convert_element_type.76, () %tuple.32, (f32[4,5,6]{2,0,1:T(4,128)S(1)}, f32[1,384]{1,0:T(1,128)S(1)}, f32[32,1]{0,1:T(1,128)S(1)}, bf16[52,404]{1,0:T(8,128)(2,1)S(1)}, bf16[5,21,21]{2,1,0:T(8,128)(2,1)S(1)}) %tuple.327), branch_computations={%region_0.1_spmd, %region_1.2_spmd} | conditional | flops 470078048 | bytes 36717480 | solution.py:108
  397.5 1.3 convert_bitcast_fusion
  398.8 3.9 copy.9
  402.7 8.9 %reshape.482 = bf16[21,148,640]{2,1,0:T(8,128)(2,1)} reshape(bf16[21,148,5,128]{3,2,1,0:T(8,128)(2,1)} %copy.9) | data formatting | bytes 7956480 | tf_op jit(solution)/shard_map/cond/branch_1_fun/reshape | solution.py:40
  411.6 8.8 %dot_general.18 = bf16[5,128,21,148]{1,0,3,2:T(8,128)(2,1)} reshape(bf16[640,21,148]{0,2,1:T(8,128)(2,1)} %bitcast.692) | data formatting | bytes 7956480 | tf_op jit(solution)/shard_map/cond/branch_1_fun/jarc,acn->jrn/dot_general | solution.py:41
  420.9 3.8 fusion.5
  426.4 6.2 %multiply_bitcast_fusion.4 = (f32[32]{0:T(128)S(1)}, f32[32]{0:T(128)S(1)}, f32[32]{0:T(128)S(1)}, f32[32]{0:T(128)S(1)}, f32[32]{0:T(128)S(1)}, /*index=5*/f32[...) fusion(f32[32,1]{0,1:T(1,128)S(1)} %get-tuple-element.48, f32[]{:T(128)} %bitcast.2, ...), kind=kLoop, calls=%fused_computation.82 | loop fusion | flops 480 | bytes 1448 | tf_op jit(solution)/shard_map/cond/branch_1_fun/add | solution.py:95
  432.7 11.2 %add_reduce_fusion.4 = (f32[384]{0:T(512)S(1)}, f32[384]{0:T(512)S(1)}, f32[384]{0:T(512)S(1)}, f32[384]{0:T(512)S(1)}, f32[384]{0:T(512)S(1)}, /*index=5*/f32[3...) fusion(f32[1,384]{1,0:T(1,128)S(1)} %get-tuple-element.47, ...), kind=kLoop, calls=%fused_computation.67 | loop fusion | flops 8448 | bytes 21576 | tf_op jit(solution)/shard_map/cond/branch_1_fun/add | solution.py:95
  443.9 1.3 fusion.18
  445.6 1.9 collective-permute-start.9
  447.5 2.4 collective-permute-start.8
  450.6 4.1 collective-permute-done.8
  454.7 13.3 %fusion.119 = f32[32,384]{1,0:T(8,128)S(1)} fusion(f32[32,384]{1,0:T(8,128)S(1)} %add_divide_fusion, f32[32,10]{1,0:T(8,128)S(1)} %collective-permute-done.9, f32[32,10]{1,0:T(8,128)S(1)} %collective-permute-done.8, f32[]{:T(128)} %bitcast.344, f32[]{:T(128)} %bitcast.343, f32[]{:T(128)} %bitcast.342, f32[]{:T(128)} %bitcast.341, f32[]{:T(128)} %bitcast.340, ...), kind=kLoop, calls=%fused_computation.427 | loop fusion | flops 749568 | bytes 100948 | tf_op jit(solution)/shard_map/add | solution.py:117
  468.0 1.9 collective-permute-start.11
  469.9 3.9 collective-permute-start.10
  473.9 7.8 %collective-permute-done.10 = f32[10,384]{1,0:T(8,128)S(1)} collective-permute-done((f32[10,384]{1,0:T(8,128)S(1)}, f32[10,384]{1,0:T(8,128)S(1)}, u32[]{:S(2)}, u32[]{:S(2)}) %collective-permute-start.10) | collective-permute-done | bytes 15392 | tf_op jit(solution)/shard_map/ppermute | solution.py:15
  481.7 13.7 %fusion.175 = f32[32,384]{1,0:T(8,128)} fusion(f32[32,384]{1,0:T(8,128)S(1)} %fusion.119, f32[10,384]{1,0:T(8,128)S(1)} %collective-permute-done.11, f32[10,384]{1,0:T(8,128)S(1)} %collective-permute-done.10, f32[]{:T(128)} %bitcast.344, f32[]{:T(128)} %bitcast.343, f32[]{:T(128)} %bitcast.342, f32[]{:T(128)} %bitcast.341, f32[]{:T(128)} %bitcast.340, ...), kind=kLoop, calls=%fused_computation.483 | loop fusion | flops 749568 | bytes 129108 | tf_op jit(solution)/shard_map/add | solution.py:121
  (167 shorter events, 11.8 us)
Async XLA Ops:
  0.6 228.1 %copy-start.4 = (f32[4]{0:T(128)S(1)}, f32[4]{0:T(128)}, u32[]{:S(2)}) copy-start(f32[4]{0:T(128)} %param.18) | copy-start | bytes 52
  0.6 228.8 %copy-start.3 = (f32[21]{0:T(128)S(1)}, f32[21]{0:T(128)}, u32[]{:S(2)}) copy-start(f32[21]{0:T(128)} %param.21) | copy-start | bytes 256
  0.7 252.2 %copy-start.1 = (f32[4,5,6]{2,0,1:T(4,128)S(1)}, f32[4,5,6]{2,0,1:T(4,128)}, u32[]{:S(2)}) copy-start(f32[4,5,6]{2,0,1:T(4,128)} %param.17) | copy-start | bytes 1444
  0.7 252.2 %copy-start = (bf16[5,21,21]{2,1,0:T(8,128)(2,1)S(1)}, bf16[5,21,21]{2,1,0:T(8,128)(2,1)}, u32[]{:S(2)}) copy-start(bf16[5,21,21]{2,1,0:T(8,128)(2,1)} %param.16) | copy-start | bytes 13234
  57.7 180.0 %collective-permute-start.7 = (bf16[52,10]{1,0:T(8,128)(2,1)S(1)}, bf16[52,10]{1,0:T(8,128)(2,1)S(1)}, u32[]{:S(2)}, u32[]{:S(2)}) collective-permute-start(bf16[52,10]{1,0:T(8,128)(2,1)S(1)} %get-tuple-element.349), channel_id=1, source_target_pairs={{16,0},{32,16},{48,32},{64,48},{80,64},{96,80},{112,96},{128,112},... | collective-permute-start | bytes 3128 | tf_op jit(solution)/shard_map/ppermute | solution.py:16
  59.7 180.0 %collective-permute-start.6 = (bf16[52,10]{1,0:T(8,128)(2,1)S(1)}, bf16[52,10]{1,0:T(8,128)(2,1)S(1)}, u32[]{:S(2)}, u32[]{:S(2)}) collective-permute-start(bf16[52,10]{1,0:T(8,128)(2,1)S(1)} %get-tuple-element.348), channel_id=1, source_target_pairs={{0,16},{16,32},{32,48},{48,64},{64,80},{80,96},{96,112},{112,128},... | collective-permute-start | bytes 3128 | tf_op jit(solution)/shard_map/ppermute | solution.py:15
  219.0 26.6 %collective-permute-start.5 = (bf16[52,10]{1,0:T(8,128)(2,1)S(1)}, bf16[52,10]{1,0:T(8,128)(2,1)S(1)}, u32[]{:S(2)}, u32[]{:S(2)}) collective-permute-start(bf16[52,10]{1,0:T(8,128)(2,1)S(1)} %get-tuple-element.347), channel_id=1, source_target_pairs={{16,0},{32,16},{48,32},{64,48},{80,64},{96,80},{112,96},{128,112},... | collective-permute-start | bytes 3128 | tf_op jit(solution)/shard_map/ppermute | solution.py:16
  220.9 26.6 %collective-permute-start.4 = (bf16[52,10]{1,0:T(8,128)(2,1)S(1)}, bf16[52,10]{1,0:T(8,128)(2,1)S(1)}, u32[]{:S(2)}, u32[]{:S(2)}) collective-permute-start(bf16[52,10]{1,0:T(8,128)(2,1)S(1)} %get-tuple-element.346), channel_id=1, source_target_pairs={{0,16},{16,32},{32,48},{48,64},{64,80},{80,96},{96,112},{112,128},... | collective-permute-start | bytes 3128 | tf_op jit(solution)/shard_map/ppermute | solution.py:15
  223.4 24.2 %collective-permute-start.3 = (bf16[52,10]{1,0:T(8,128)(2,1)S(1)}, bf16[52,10]{1,0:T(8,128)(2,1)S(1)}, u32[]{:S(2)}, u32[]{:S(2)}) collective-permute-start(bf16[52,10]{1,0:T(8,128)(2,1)S(1)} %get-tuple-element.345), channel_id=1, source_target_pairs={{16,0},{32,16},{48,32},{64,48},{80,64},{96,80},{112,96},{128,112},... | collective-permute-start | bytes 3128 | tf_op jit(solution)/shard_map/ppermute | solution.py:16
  237.8 9.9 %collective-permute-start.2 = (bf16[52,10]{1,0:T(8,128)(2,1)S(1)}, bf16[52,10]{1,0:T(8,128)(2,1)S(1)}, u32[]{:S(2)}, u32[]{:S(2)}) collective-permute-start(bf16[52,10]{1,0:T(8,128)(2,1)S(1)} %get-tuple-element.344), channel_id=1, source_target_pairs={{0,16},{16,32},{32,48},{48,64},{64,80},{80,96},{96,112},{112,128},... | collective-permute-start | bytes 3128 | tf_op jit(solution)/shard_map/ppermute | solution.py:15
  239.7 8.0 %collective-permute-start.1 = (bf16[52,10]{1,0:T(8,128)(2,1)S(1)}, bf16[52,10]{1,0:T(8,128)(2,1)S(1)}, u32[]{:S(2)}, u32[]{:S(2)}) collective-permute-start(bf16[52,10]{1,0:T(8,128)(2,1)S(1)} %get-tuple-element.340), channel_id=1, source_target_pairs={{16,0},{32,16},{48,32},{64,48},{80,64},{96,80},{112,96},{128,112},... | collective-permute-start | bytes 3128 | tf_op jit(solution)/shard_map/ppermute | solution.py:16
  245.6 7.1 %collective-permute-start = (bf16[52,10]{1,0:T(8,128)(2,1)S(1)}, bf16[52,10]{1,0:T(8,128)(2,1)S(1)}, u32[]{:S(2)}, u32[]{:S(2)}) collective-permute-start(bf16[52,10]{1,0:T(8,128)(2,1)S(1)} %get-tuple-element.339), channel_id=1, source_target_pairs={{0,16},{16,32},{32,48},{48,64},{64,80},{80,96},{96,112},{112,128},... | collective-permute-start | bytes 3128 | tf_op jit(solution)/shard_map/ppermute | solution.py:15
  445.5 49.9 %copy-start.2 = (f32[32,384]{1,0:T(8,128)}, f32[32,384]{1,0:T(8,128)S(1)}, u32[]{:S(2)}) copy-start(f32[32,384]{1,0:T(8,128)S(1)} %add_divide_fusion) | copy-start | bytes 147460
  445.6 5.0 %collective-permute-start.9 = (f32[32,10]{1,0:T(8,128)S(1)}, f32[32,10]{1,0:T(8,128)S(1)}, u32[]{:S(2)}, u32[]{:S(2)}) collective-permute-start(f32[32,10]{1,0:T(8,128)S(1)} %get-tuple-element.338), channel_id=1, source_target_pairs={{16,0},{32,16},{48,32},{64,48},{80,64},{96,80},{112,96},{128,112},... | collective-permute-start | bytes 3848 | tf_op jit(solution)/shard_map/ppermute | solution.py:16
  447.5 7.2 %collective-permute-start.8 = (f32[32,10]{1,0:T(8,128)S(1)}, f32[32,10]{1,0:T(8,128)S(1)}, u32[]{:S(2)}, u32[]{:S(2)}) collective-permute-start(f32[32,10]{1,0:T(8,128)S(1)} %get-tuple-element.337), channel_id=1, source_target_pairs={{0,16},{16,32},{32,48},{48,64},{64,80},{80,96},{96,112},{112,128},... | collective-permute-start | bytes 3848 | tf_op jit(solution)/shard_map/ppermute | solution.py:15
  468.0 5.9 %collective-permute-start.11 = (f32[10,384]{1,0:T(8,128)S(1)}, f32[10,384]{1,0:T(8,128)S(1)}, u32[]{:S(2)}, u32[]{:S(2)}) collective-permute-start(f32[10,384]{1,0:T(8,128)S(1)} %get-tuple-element.336), channel_id=1, source_target_pairs={{1,0},{2,1},{3,2},{4,3},{5,4},{6,5},{7,6},{8,7},{9,8},{10,9},{11,1... | collective-permute-start | bytes 46088 | tf_op jit(solution)/shard_map/ppermute | solution.py:16
  469.9 11.7 %collective-permute-start.10 = (f32[10,384]{1,0:T(8,128)S(1)}, f32[10,384]{1,0:T(8,128)S(1)}, u32[]{:S(2)}, u32[]{:S(2)}) collective-permute-start(f32[10,384]{1,0:T(8,128)S(1)} %get-tuple-element.335), channel_id=1, source_target_pairs={{0,1},{1,2},{2,3},{3,4},{4,5},{5,6},{6,7},{7,8},{8,9},{9,10},{10,1... | collective-permute-start | bytes 46088 | tf_op jit(solution)/shard_map/ppermute | solution.py:15
where the time goes:
time: 499 us; the launch traced here: 495 us
  blocking collectives  199 us (40%)
  other arithmetic  111 us (22%)
  local copies, waits for them, and re-layouts  100 us (20%)
  starting transfers between devices  33.6 us (7%)
  matrix products  20.7 us (4%)
  waiting for transfers between devices  16.9 us (3%)
  between operations  11.2 us (2%)
    all_gather x4, blocking collectives, on_device(): lax.all_gather(exposures[member], 'narrow', axis=0, tiled=True)  199 us
    add x8, other arithmetic, matched_tile(): coeffs[0] + coeffs[1] * x_coord + coeffs[2] * y_coord  69.9 us
    reshape x4, local copies, waits for them, and re-layouts, respond(): table = table.astype(jnp.bfloat16).reshape(side, span, kernel_total * block)  35.6 us
    dot_general x4, local copies, waits for them, and re-layouts, respond(): jnp.einsum('jarc,acn->jrn', patches, table, preferred_element_type=jnp.fl...  35.1 us
    ppermute x6, starting transfers between devices, padded(): after = lax.ppermute(initial, axis, down)  18.7 us
    ppermute x6, waiting for transfers between devices, padded(): before = lax.ppermute(last, axis, up)  16.9 us
    convert_element_type x4, local copies, waits for them, and re-layouts, respond(): table = table.astype(jnp.bfloat16).reshape(side, span, kernel_total * block)  15.6 us
    dot_general x4, matrix products, respond(): jnp.einsum('jarc,acn->jrn', patches, table, preferred_element_type=jnp.fl...  15.4 us
  transfers between devices with their start and end apart: 12, of which 3 were waited for; matrix products, arithmetic and copies ran while one was open for 2% of the time, Pallas kernels for 0%

commit v1 on v0

--- a/solution.py
+++ b/solution.py
@@ -3,6 +3,11 @@
 import jax.numpy as jnp
 from jax import lax
 from jax.sharding import PartitionSpec as P
+
+cycles_answer = lambda frame, axis_name: jnp.concatenate(
+    lax.all_to_all(jnp.stack([frame for _ in range(lax.axis_size(axis_name))], 0), axis_name, 0, 0),
+    0,
+)
 
 
 def padded(array, sides, width):
@@ -75,11 +80,7 @@
             return jnp.where(present[:, None], sliced, window)
 
         empty_window = jnp.zeros((tile_rows + 20, tile_cols), exposures.dtype)
-        window = placed_rows(
-            empty_window,
-            lax.all_gather(exposures[member], "narrow", axis=0, tiled=True),
-            jnp.int32(0),
-        )
+        window = placed_rows(empty_window, cycles_answer(exposures[member], "narrow"), jnp.int32(0))
         window_rows = row_base - 10 + jnp.arange(tile_rows + 20, dtype=jnp.int32)
         valid_rows = (window_rows >= first_row) & (window_rows < first_row + row_total)
         window = jnp.where(valid_rows[:, None], window, zero_value)

time: 499 us -> 368 us (0.74)
  the two profiles are of different devices: /device:TPU:384 before, /device:TPU:448 now
where the time goes in v1:
time: 368 us; the launch traced here: 364 us
  other arithmetic  111 us (30%)
  local copies, waits for them, and re-layouts  104 us (28%)
  starting transfers between devices  68.8 us (19%)
  blocking collectives  24.1 us (7%)
  waiting for transfers between devices  22.5 us (6%)
  matrix products  20.7 us (6%)
  between operations  11.2 us (3%)
    add x8, other arithmetic, matched_tile(): coeffs[0] + coeffs[1] * x_coord + coeffs[2] * y_coord  69.8 us
    reshape x4, local copies, waits for them, and re-layouts, respond(): table = table.astype(jnp.bfloat16).reshape(side, span, kernel_total * block)  35.6 us
    dot_general x4, local copies, waits for them, and re-layouts, respond(): jnp.einsum('jarc,acn->jrn', patches, table, preferred_element_type=jnp.fl...  35.1 us
    all_to_all x3, starting transfers between devices, lax.all_to_all(jnp.stack([frame for _ in range(lax.axis_size(axis_name))]...  30.6 us
    ppermute x6, starting transfers between devices, padded(): after = lax.ppermute(initial, axis, down)  24.2 us
    all_to_all x1, blocking collectives, lax.all_to_all(jnp.stack([frame for _ in range(lax.axis_size(axis_name))]...  24.1 us
    ppermute x6, waiting for transfers between devices, padded(): before = lax.ppermute(last, axis, up)  16.9 us
    convert_element_type x4, local copies, waits for them, and re-layouts, respond(): table = table.astype(jnp.bfloat16).reshape(side, span, kernel_total * block)  15.6 us
  transfers between devices with their start and end apart: 15, of which 5 were waited for; matrix products, arithmetic and copies ran while one was open for 4% of the time, Pallas kernels for 0%

profile of v1, /device:TPU:448, one launch (start us, length us, event | category | flops | bytes accessed | tf_op | source)
XLA Modules:
  0.0 363.7 jit_solution(12662371495738432425)
XLA Ops:
  0.7 0.8 slice_bitcast_fusion.15
  1.5 24.1 %all_to_all.20 = bf16[16,32,384]{2,1,0:T(8,128)(2,1)S(1)} all-to-all(bf16[16,32,384]{2,1,0:T(8,128)(2,1)S(1)} %stack.327), channel_id=1, replica_groups=mesh['wide'=32,'narrow'=16] {'narrow'}, dimensions={0} | all-to-all | bytes 786432 | tf_op jit(solution)/shard_map/all_to_all | solution.py:8
  26.4 9.5 %all-to-all-start = ((bf16[16,32,384]{2,1,0:T(8,128)(2,1)}), bf16[16,32,384]{2,1,0:T(8,128)(2,1)S(1)}, u32[]{:S(2)}, u32[]{:S(2)}) async-start(bf16[16,32,384]{2,1,0:T(8,128)(2,1)} %stack.324), calls=%async_computation | async-start | bytes 786432 | tf_op jit(solution)/shard_map/all_to_all | solution.py:8
  36.0 1.5 fusion.262
  42.5 5.1 %all-to-all-done = bf16[16,32,384]{2,1,0:T(8,128)(2,1)S(1)} async-done(((bf16[16,32,384]{2,1,0:T(8,128)(2,1)}), bf16[16,32,384]{2,1,0:T(8,128)(2,1)S(1)}, u32[]{:S(2)}, u32[]{:S(2)}) %all-to-all-start) | async-done | bytes 393248 | tf_op jit(solution)/shard_map/all_to_all | solution.py:8
  48.3 9.5 %all-to-all-start.1 = ((bf16[16,32,384]{2,1,0:T(8,128)(2,1)}), bf16[16,32,384]{2,1,0:T(8,128)(2,1)S(1)}, u32[]{:S(2)}, u32[]{:S(2)}) async-start(bf16[16,32,384]{2,1,0:T(8,128)(2,1)} %stack.325), calls=%async_computation.1 | async-start | bytes 786432 | tf_op jit(solution)/shard_map/all_to_all | solution.py:8
  57.8 1.5 fusion.261
  65.8 1.2 compare_and_fusion.3
  67.0 1.5 fusion.260
  69.8 11.5 %all-to-all-start.2 = ((bf16[16,32,384]{2,1,0:T(8,128)(2,1)}), bf16[16,32,384]{2,1,0:T(8,128)(2,1)S(1)}, u32[]{:S(2)}, u32[]{:S(2)}) async-start(bf16[16,32,384]{2,1,0:T(8,128)(2,1)} %stack.326), calls=%async_computation.2 | async-start | bytes 786432 | tf_op jit(solution)/shard_map/all_to_all | solution.py:8
  81.3 5.0 %add_add_fusion = (f32[32]{0:T(128)S(1)}, f32[32]{0:T(128)S(1)}, f32[32]{0:T(128)S(1)}, f32[32]{0:T(128)S(1)}, f32[32]{0:T(128)S(1)}) fusion(f32[]{:T(128)} %bitcast.315, s32[]{:T(128)S(6)} %add.1350, s32[]{:T(128)} %bitcast.313, s32[]{:T(128)S(6)} %mul.1366, f32[]{:T(128)} %bitcast.310, s32[]{:T(128)S(6)} %add.1334, s32[]{:T(128)} %bitcast.308, ...), kind=kLoop, calls=%fused_computation.574 | loop fusion | flops 640 | bytes 692 | tf_op jit(solution)/shard_map/add | solution.py:112
  87.2 3.1 collective-permute-start.7
  90.4 1.9 collective-permute-start.6
  92.7 5.7 %collective-permute-start.5 = (bf16[52,10]{1,0:T(8,128)(2,1)S(1)}, bf16[52,10]{1,0:T(8,128)(2,1)S(1)}, u32[]{:S(2)}, u32[]{:S(2)}) collective-permute-start(bf16[52,10]{1,0:T(8,128)(2,1)S(1)} %get-tuple-element.347), channel_id=1, source_target_pairs={{16,0},{32,16},{48,32},{64,48},{80,64},{96,80},{112,96},{128,112},... | collective-permute-start | bytes 3128 | tf_op jit(solution)/shard_map/ppermute | solution.py:21
  98.5 1.9 collective-permute-start.4
  100.5 5.7 %collective-permute-start.3 = (bf16[52,10]{1,0:T(8,128)(2,1)S(1)}, bf16[52,10]{1,0:T(8,128)(2,1)S(1)}, u32[]{:S(2)}, u32[]{:S(2)}) collective-permute-start(bf16[52,10]{1,0:T(8,128)(2,1)S(1)} %get-tuple-element.345), channel_id=1, source_target_pairs={{16,0},{32,16},{48,32},{64,48},{80,64},{96,80},{112,96},{128,112},... | collective-permute-start | bytes 3128 | tf_op jit(solution)/shard_map/ppermute | solution.py:21
  106.3 1.9 collective-permute-start.2
  108.2 5.8 %collective-permute-start.1 = (bf16[52,10]{1,0:T(8,128)(2,1)S(1)}, bf16[52,10]{1,0:T(8,128)(2,1)S(1)}, u32[]{:S(2)}, u32[]{:S(2)}) collective-permute-start(bf16[52,10]{1,0:T(8,128)(2,1)S(1)} %get-tuple-element.340), channel_id=1, source_target_pairs={{16,0},{32,16},{48,32},{64,48},{80,64},{96,80},{112,96},{128,112},... | collective-permute-start | bytes 3128 | tf_op jit(solution)/shard_map/ppermute | solution.py:21
  114.1 1.9 collective-permute-start
  116.3 5.0 %collective-permute-done = bf16[52,10]{1,0:T(8,128)(2,1)S(1)} collective-permute-done((bf16[52,10]{1,0:T(8,128)(2,1)S(1)}, bf16[52,10]{1,0:T(8,128)(2,1)S(1)}, u32[]{:S(2)}, u32[]{:S(2)}) %collective-permute-start) | collective-permute-done | bytes 1072 | tf_op jit(solution)/shard_map/ppermute | solution.py:20
  121.4 47.9 %conditional.7 = (f32[32,384]{1,0:T(8,128)S(1)}) conditional(s32[]{:T(128)} %convert_element_type.81, () %tuple.38, (f32[4,5,6]{2,0,1:T(4,128)S(1)}, f32[1,384]{1,0:T(1,128)S(1)}, f32[32,1]{0,1:T(1,128)S(1)}, bf16[52,404]{1,0:T(8,128)(2,1)S(1)}, bf16[5,21,21]{2,1,0:T(8,128)(2,1)S(1)}) %tuple.324), branch_computations={%region_6.7_spmd, %region_7.8_spmd} | conditional | flops 470078048 | bytes 36717480 | solution.py:109
  121.4 1.3 convert_bitcast_fusion.3
  122.7 3.9 %copy.30 = bf16[21,148,5,128]{3,2,1,0:T(8,128)(2,1)} copy(bf16[21,148,5,128]{3,0,2,1:T(8,128)(2,1)S(1)} %convert_bitcast_fusion.3) | data formatting | bytes 7956480 | tf_op jit(solution)/shard_map/cond/branch_1_fun/convert_element_type | solution.py:45
  126.6 8.9 %reshape.497 = bf16[21,148,640]{2,1,0:T(8,128)(2,1)} reshape(bf16[21,148,5,128]{3,2,1,0:T(8,128)(2,1)} %copy.30) | data formatting | bytes 7956480 | tf_op jit(solution)/shard_map/cond/branch_1_fun/reshape | solution.py:45
  135.5 8.8 %dot_general.38 = bf16[5,128,21,148]{1,0,3,2:T(8,128)(2,1)} reshape(bf16[640,21,148]{0,2,1:T(8,128)(2,1)} %bitcast.697) | data formatting | bytes 7956480 | tf_op jit(solution)/shard_map/cond/branch_1_fun/jarc,acn->jrn/dot_general | solution.py:46
  144.8 3.8 %fusion.92 = f32[5,32,3,128]{3,1,0,2:T(8,128)S(1)} fusion(bf16[5,128,21,148]{1,0,3,2:T(8,128)(2,1)} %dot_general.38, bf16[1,21,32,148]{3,2,1,0:T(8,128)(2,1)S(1)} %get-tuple-element.284, bf16[1,21,32,148]{3,2,1,0:T(8,128)(2,1)S(1)} %get-tuple-element.285, bf16[1,21,32,148]{3,2,1,0:T(8,128)(2,1)S(1)} %get-tuple-element.283), kind=kOutput, calls=%fused_computation.258 | convolution fusion | flops 383701248 | bytes 4820736 | tf_op jit(solution)/shard_map/cond/branch_1_fun/jarc,acn->jrn/dot_general | solution.py:46
  150.4 6.2 %multiply_bitcast_fusion.19 = (f32[32]{0:T(128)S(1)}, f32[32]{0:T(128)S(1)}, f32[32]{0:T(128)S(1)}, f32[32]{0:T(128)S(1)}, f32[32]{0:T(128)S(1)}, /*index=5*/f32...) fusion(f32[32,1]{0,1:T(1,128)S(1)} %get-tuple-element.69, f32[]{:T(128)} %bitcast.233, ...), kind=kLoop, calls=%fused_computation.334 | loop fusion | flops 480 | bytes 1448 | tf_op jit(solution)/shard_map/cond/branch_1_fun/add | solution.py:96
  156.6 11.2 %add_reduce_fusion.19 = (f32[384]{0:T(512)S(1)}, f32[384]{0:T(512)S(1)}, f32[384]{0:T(512)S(1)}, f32[384]{0:T(512)S(1)}, f32[384]{0:T(512)S(1)}, /*index=5*/f32[...) fusion(f32[1,384]{1,0:T(1,128)S(1)} %get-tuple-element.68, ...), kind=kLoop, calls=%fused_computation.319 | loop fusion | flops 8448 | bytes 21576 | tf_op jit(solution)/shard_map/cond/branch_1_fun/add | solution.py:96
  167.8 1.3 fusion.105
  169.3 48.1 %conditional.6 = (f32[32,384]{1,0:T(8,128)S(1)}) conditional(s32[]{:T(128)} %convert_element_type.80, () %tuple.36, (f32[4,5,6]{2,0,1:T(4,128)S(1)}, f32[1,384]{1,0:T(1,128)S(1)}, f32[32,1]{0,1:T(1,128)S(1)}, bf16[52,404]{1,0:T(8,128)(2,1)S(1)}, bf16[5,21,21]{2,1,0:T(8,128)(2,1)S(1)}) %tuple.325), branch_computations={%region_4.5_spmd, %region_5.6_spmd} | conditional | flops 470078048 | bytes 36717480 | solution.py:109
  169.5 1.3 convert_bitcast_fusion.2
  170.9 3.9 %copy.23 = bf16[21,148,5,128]{3,2,1,0:T(8,128)(2,1)} copy(bf16[21,148,5,128]{3,0,2,1:T(8,128)(2,1)S(1)} %convert_bitcast_fusion.2) | data formatting | bytes 7956480 | tf_op jit(solution)/shard_map/cond/branch_1_fun/convert_element_type | solution.py:45
  174.8 8.9 %reshape.496 = bf16[21,148,640]{2,1,0:T(8,128)(2,1)} reshape(bf16[21,148,5,128]{3,2,1,0:T(8,128)(2,1)} %copy.23) | data formatting | bytes 7956480 | tf_op jit(solution)/shard_map/cond/branch_1_fun/reshape | solution.py:45
  183.7 8.8 %dot_general.34 = bf16[5,128,21,148]{1,0,3,2:T(8,128)(2,1)} reshape(bf16[640,21,148]{0,2,1:T(8,128)(2,1)} %bitcast.698) | data formatting | bytes 7956480 | tf_op jit(solution)/shard_map/cond/branch_1_fun/jarc,acn->jrn/dot_general | solution.py:46
  193.0 3.8 %fusion.63 = f32[5,32,3,128]{3,1,0,2:T(8,128)S(1)} fusion(bf16[5,128,21,148]{1,0,3,2:T(8,128)(2,1)} %dot_general.34, bf16[1,21,32,148]{3,2,1,0:T(8,128)(2,1)S(1)} %get-tuple-element.236, bf16[1,21,32,148]{3,2,1,0:T(8,128)(2,1)S(1)} %get-tuple-element.237, bf16[1,21,32,148]{3,2,1,0:T(8,128)(2,1)S(1)} %get-tuple-element.235), kind=kOutput, calls=%fused_computation.174 | convolution fusion | flops 383701248 | bytes 4820736 | tf_op jit(solution)/shard_map/cond/branch_1_fun/jarc,acn->jrn/dot_general | solution.py:46
  198.5 6.2 %multiply_bitcast_fusion.14 = (f32[32]{0:T(128)S(1)}, f32[32]{0:T(128)S(1)}, f32[32]{0:T(128)S(1)}, f32[32]{0:T(128)S(1)}, f32[32]{0:T(128)S(1)}, /*index=5*/f32...) fusion(f32[32,1]{0,1:T(1,128)S(1)} %get-tuple-element.64, f32[]{:T(128)} %bitcast.156, ...), kind=kLoop, calls=%fused_computation.250 | loop fusion | flops 480 | bytes 1448 | tf_op jit(solution)/shard_map/cond/branch_1_fun/add | solution.py:96
  204.7 11.2 %add_reduce_fusion.14 = (f32[384]{0:T(512)S(1)}, f32[384]{0:T(512)S(1)}, f32[384]{0:T(512)S(1)}, f32[384]{0:T(512)S(1)}, f32[384]{0:T(512)S(1)}, /*index=5*/f32[...) fusion(f32[1,384]{1,0:T(1,128)S(1)} %get-tuple-element.63, ...), kind=kLoop, calls=%fused_computation.235 | loop fusion | flops 8448 | bytes 21576 | tf_op jit(solution)/shard_map/cond/branch_1_fun/add | solution.py:96
  215.9 1.3 fusion.76
  217.4 48.2 %conditional.5 = (f32[32,384]{1,0:T(8,128)S(1)}) conditional(s32[]{:T(128)} %convert_element_type.79, () %tuple.34, (f32[4,5,6]{2,0,1:T(4,128)S(1)}, f32[1,384]{1,0:T(1,128)S(1)}, f32[32,1]{0,1:T(1,128)S(1)}, bf16[52,404]{1,0:T(8,128)(2,1)S(1)}, bf16[5,21,21]{2,1,0:T(8,128)(2,1)S(1)}) %tuple.326), branch_computations={%region_2.3_spmd, %region_3.4_spmd} | conditional | flops 470078048 | bytes 36717480 | solution.py:109
  217.7 1.3 convert_bitcast_fusion.1
  219.0 3.9 %copy.16 = bf16[21,148,5,128]{3,2,1,0:T(8,128)(2,1)} copy(bf16[21,148,5,128]{3,0,2,1:T(8,128)(2,1)S(1)} %convert_bitcast_fusion.1) | data formatting | bytes 7956480 | tf_op jit(solution)/shard_map/cond/branch_1_fun/convert_element_type | solution.py:45
  222.9 8.9 %reshape.495 = bf16[21,148,640]{2,1,0:T(8,128)(2,1)} reshape(bf16[21,148,5,128]{3,2,1,0:T(8,128)(2,1)} %copy.16) | data formatting | bytes 7956480 | tf_op jit(solution)/shard_map/cond/branch_1_fun/reshape | solution.py:45
  231.8 8.8 %dot_general.26 = bf16[5,128,21,148]{1,0,3,2:T(8,128)(2,1)} reshape(bf16[640,21,148]{0,2,1:T(8,128)(2,1)} %bitcast.699) | data formatting | bytes 7956480 | tf_op jit(solution)/shard_map/cond/branch_1_fun/jarc,acn->jrn/dot_general | solution.py:46
  241.1 3.8 %fusion.34 = f32[5,32,3,128]{3,1,0,2:T(8,128)S(1)} fusion(bf16[5,128,21,148]{1,0,3,2:T(8,128)(2,1)} %dot_general.26, bf16[1,21,32,148]{3,2,1,0:T(8,128)(2,1)S(1)} %get-tuple-element.188, bf16[1,21,32,148]{3,2,1,0:T(8,128)(2,1)S(1)} %get-tuple-element.189, bf16[1,21,32,148]{3,2,1,0:T(8,128)(2,1)S(1)} %get-tuple-element.187), kind=kOutput, calls=%fused_computation.90 | convolution fusion | flops 383701248 | bytes 4820736 | tf_op jit(solution)/shard_map/cond/branch_1_fun/jarc,acn->jrn/dot_general | solution.py:46
  246.6 6.2 %multiply_bitcast_fusion.9 = (f32[32]{0:T(128)S(1)}, f32[32]{0:T(128)S(1)}, f32[32]{0:T(128)S(1)}, f32[32]{0:T(128)S(1)}, f32[32]{0:T(128)S(1)}, /*index=5*/f32[...) fusion(f32[32,1]{0,1:T(1,128)S(1)} %get-tuple-element.59, f32[]{:T(128)} %bitcast.79, ...), kind=kLoop, calls=%fused_computation.166 | loop fusion | flops 480 | bytes 1448 | tf_op jit(solution)/shard_map/cond/branch_1_fun/add | solution.py:96
  252.9 11.2 %add_reduce_fusion.9 = (f32[384]{0:T(512)S(1)}, f32[384]{0:T(512)S(1)}, f32[384]{0:T(512)S(1)}, f32[384]{0:T(512)S(1)}, f32[384]{0:T(512)S(1)}, /*index=5*/f32[3...) fusion(f32[1,384]{1,0:T(1,128)S(1)} %get-tuple-element.58, ...), kind=kLoop, calls=%fused_computation.151 | loop fusion | flops 8448 | bytes 21576 | tf_op jit(solution)/shard_map/cond/branch_1_fun/add | solution.py:96
  264.1 1.3 fusion.47
  265.6 48.2 %conditional.4 = (f32[32,384]{1,0:T(8,128)S(1)}) conditional(s32[]{:T(128)} %convert_element_type.76, () %tuple.32, (f32[4,5,6]{2,0,1:T(4,128)S(1)}, f32[1,384]{1,0:T(1,128)S(1)}, f32[32,1]{0,1:T(1,128)S(1)}, bf16[52,404]{1,0:T(8,128)(2,1)S(1)}, bf16[5,21,21]{2,1,0:T(8,128)(2,1)S(1)}) %tuple.327), branch_computations={%region_0.1_spmd, %region_1.2_spmd} | conditional | flops 470078048 | bytes 36717480 | solution.py:109
  265.9 1.3 convert_bitcast_fusion
  267.2 3.9 %copy.9 = bf16[21,148,5,128]{3,2,1,0:T(8,128)(2,1)} copy(bf16[21,148,5,128]{3,0,2,1:T(8,128)(2,1)S(1)} %convert_bitcast_fusion) | data formatting | bytes 7956480 | tf_op jit(solution)/shard_map/cond/branch_1_fun/convert_element_type | solution.py:45
  271.1 8.9 %reshape.494 = bf16[21,148,640]{2,1,0:T(8,128)(2,1)} reshape(bf16[21,148,5,128]{3,2,1,0:T(8,128)(2,1)} %copy.9) | data formatting | bytes 7956480 | tf_op jit(solution)/shard_map/cond/branch_1_fun/reshape | solution.py:45
  280.0 8.8 %dot_general.18 = bf16[5,128,21,148]{1,0,3,2:T(8,128)(2,1)} reshape(bf16[640,21,148]{0,2,1:T(8,128)(2,1)} %bitcast.700) | data formatting | bytes 7956480 | tf_op jit(solution)/shard_map/cond/branch_1_fun/jarc,acn->jrn/dot_general | solution.py:46
  289.3 3.8 %fusion.5 = f32[5,32,3,128]{3,1,0,2:T(8,128)S(1)} fusion(bf16[5,128,21,148]{1,0,3,2:T(8,128)(2,1)} %dot_general.18, bf16[1,21,32,148]{3,2,1,0:T(8,128)(2,1)S(1)} %get-tuple-element.140, bf16[1,21,32,148]{3,2,1,0:T(8,128)(2,1)S(1)} %get-tuple-element.141, bf16[1,21,32,148]{3,2,1,0:T(8,128)(2,1)S(1)} %get-tuple-element.139), kind=kOutput, calls=%fused_computation.6 | convolution fusion | flops 383701248 | bytes 4820736 | tf_op jit(solution)/shard_map/cond/branch_1_fun/jarc,acn->jrn/dot_general | solution.py:46
  294.9 6.2 %multiply_bitcast_fusion.4 = (f32[32]{0:T(128)S(1)}, f32[32]{0:T(128)S(1)}, f32[32]{0:T(128)S(1)}, f32[32]{0:T(128)S(1)}, f32[32]{0:T(128)S(1)}, /*index=5*/f32[...) fusion(f32[32,1]{0,1:T(1,128)S(1)} %get-tuple-element.48, f32[]{:T(128)} %bitcast.2, ...), kind=kLoop, calls=%fused_computation.82 | loop fusion | flops 480 | bytes 1448 | tf_op jit(solution)/shard_map/cond/branch_1_fun/add | solution.py:96
  301.1 11.2 %add_reduce_fusion.4 = (f32[384]{0:T(512)S(1)}, f32[384]{0:T(512)S(1)}, f32[384]{0:T(512)S(1)}, f32[384]{0:T(512)S(1)}, f32[384]{0:T(512)S(1)}, /*index=5*/f32[3...) fusion(f32[1,384]{1,0:T(1,128)S(1)} %get-tuple-element.47, ...), kind=kLoop, calls=%fused_computation.67 | loop fusion | flops 8448 | bytes 21576 | tf_op jit(solution)/shard_map/cond/branch_1_fun/add | solution.py:96
  312.3 1.3 fusion.18
  314.0 1.9 collective-permute-start.9
  315.9 2.4 collective-permute-start.8
  319.0 4.1 %collective-permute-done.8 = f32[32,10]{1,0:T(8,128)S(1)} collective-permute-done((f32[32,10]{1,0:T(8,128)S(1)}, f32[32,10]{1,0:T(8,128)S(1)}, u32[]{:S(2)}, u32[]{:S(2)}) %collective-permute-start.8) | collective-permute-done | bytes 1312 | tf_op jit(solution)/shard_map/ppermute | solution.py:20
  323.1 13.3 %fusion.119 = f32[32,384]{1,0:T(8,128)S(1)} fusion(f32[32,384]{1,0:T(8,128)S(1)} %add_divide_fusion, f32[32,10]{1,0:T(8,128)S(1)} %collective-permute-done.9, f32[32,10]{1,0:T(8,128)S(1)} %collective-permute-done.8, f32[]{:T(128)} %bitcast.348, f32[]{:T(128)} %bitcast.347, f32[]{:T(128)} %bitcast.346, f32[]{:T(128)} %bitcast.345, f32[]{:T(128)} %bitcast.344, ...), kind=kLoop, calls=%fused_computation.427 | loop fusion | flops 749568 | bytes 100948 | tf_op jit(solution)/shard_map/add | solution.py:118
  336.4 1.9 collective-permute-start.11
  338.3 3.9 %collective-permute-start.10 = (f32[10,384]{1,0:T(8,128)S(1)}, f32[10,384]{1,0:T(8,128)S(1)}, u32[]{:S(2)}, u32[]{:S(2)}) collective-permute-start(f32[10,384]{1,0:T(8,128)S(1)} %get-tuple-element.335), channel_id=1, source_target_pairs={{0,1},{1,2},{2,3},{3,4},{4,5},{5,6},{6,7},{7,8},{8,9},{9,10},{10,1... | collective-permute-start | bytes 46088 | tf_op jit(solution)/shard_map/ppermute | solution.py:20
  342.3 7.8 %collective-permute-done.10 = f32[10,384]{1,0:T(8,128)S(1)} collective-permute-done((f32[10,384]{1,0:T(8,128)S(1)}, f32[10,384]{1,0:T(8,128)S(1)}, u32[]{:S(2)}, u32[]{:S(2)}) %collective-permute-start.10) | collective-permute-done | bytes 15392 | tf_op jit(solution)/shard_map/ppermute | solution.py:20
  350.1 13.6 %fusion.175 = f32[32,384]{1,0:T(8,128)} fusion(f32[32,384]{1,0:T(8,128)S(1)} %fusion.119, f32[10,384]{1,0:T(8,128)S(1)} %collective-permute-done.11, f32[10,384]{1,0:T(8,128)S(1)} %collective-permute-done.10, f32[]{:T(128)} %bitcast.348, f32[]{:T(128)} %bitcast.347, f32[]{:T(128)} %bitcast.346, f32[]{:T(128)} %bitcast.345, f32[]{:T(128)} %bitcast.344, ...), kind=kLoop, calls=%fused_computation.483 | loop fusion | flops 749568 | bytes 129108 | tf_op jit(solution)/shard_map/add | solution.py:122
  (172 shorter events, 15.5 us)
Async XLA Ops:
  0.6 85.6 %copy-start.3 = (f32[21]{0:T(128)S(1)}, f32[21]{0:T(128)}, u32[]{:S(2)}) copy-start(f32[21]{0:T(128)} %param.21) | copy-start | bytes 256
  0.6 120.7 %copy-start.1 = (f32[4,5,6]{2,0,1:T(4,128)S(1)}, f32[4,5,6]{2,0,1:T(4,128)}, u32[]{:S(2)}) copy-start(f32[4,5,6]{2,0,1:T(4,128)} %param.17) | copy-start | bytes 1444
  0.7 120.7 %copy-start = (bf16[5,21,21]{2,1,0:T(8,128)(2,1)S(1)}, bf16[5,21,21]{2,1,0:T(8,128)(2,1)}, u32[]{:S(2)}) copy-start(bf16[5,21,21]{2,1,0:T(8,128)(2,1)} %param.16) | copy-start | bytes 13234
  26.4 21.1 %all-to-all-start = ((bf16[16,32,384]{2,1,0:T(8,128)(2,1)}), bf16[16,32,384]{2,1,0:T(8,128)(2,1)S(1)}, u32[]{:S(2)}, u32[]{:S(2)}) async-start(bf16[16,32,384]{2,1,0:T(8,128)(2,1)} %stack.324), calls=%async_computation | async-start | bytes 786432 | tf_op jit(solution)/shard_map/all_to_all | solution.py:8
  48.3 20.7 %all-to-all-start.1 = ((bf16[16,32,384]{2,1,0:T(8,128)(2,1)}), bf16[16,32,384]{2,1,0:T(8,128)(2,1)S(1)}, u32[]{:S(2)}, u32[]{:S(2)}) async-start(bf16[16,32,384]{2,1,0:T(8,128)(2,1)} %stack.325), calls=%async_computation.1 | async-start | bytes 786432 | tf_op jit(solution)/shard_map/all_to_all | solution.py:8
  69.8 22.5 %all-to-all-start.2 = ((bf16[16,32,384]{2,1,0:T(8,128)(2,1)}), bf16[16,32,384]{2,1,0:T(8,128)(2,1)S(1)}, u32[]{:S(2)}, u32[]{:S(2)}) async-start(bf16[16,32,384]{2,1,0:T(8,128)(2,1)} %stack.326), calls=%async_computation.2 | async-start | bytes 786432 | tf_op jit(solution)/shard_map/all_to_all | solution.py:8
  87.2 19.1 %collective-permute-start.7 = (bf16[52,10]{1,0:T(8,128)(2,1)S(1)}, bf16[52,10]{1,0:T(8,128)(2,1)S(1)}, u32[]{:S(2)}, u32[]{:S(2)}) collective-permute-start(bf16[52,10]{1,0:T(8,128)(2,1)S(1)} %get-tuple-element.349), channel_id=1, source_target_pairs={{16,0},{32,16},{48,32},{64,48},{80,64},{96,80},{112,96},{128,112},... | collective-permute-start | bytes 3128 | tf_op jit(solution)/shard_map/ppermute | solution.py:21
  90.4 17.9 %collective-permute-start.6 = (bf16[52,10]{1,0:T(8,128)(2,1)S(1)}, bf16[52,10]{1,0:T(8,128)(2,1)S(1)}, u32[]{:S(2)}, u32[]{:S(2)}) collective-permute-start(bf16[52,10]{1,0:T(8,128)(2,1)S(1)} %get-tuple-element.348), channel_id=1, source_target_pairs={{0,16},{16,32},{32,48},{48,64},{64,80},{80,96},{96,112},{112,128},... | collective-permute-start | bytes 3128 | tf_op jit(solution)/shard_map/ppermute | solution.py:20
  92.7 21.4 %collective-permute-start.5 = (bf16[52,10]{1,0:T(8,128)(2,1)S(1)}, bf16[52,10]{1,0:T(8,128)(2,1)S(1)}, u32[]{:S(2)}, u32[]{:S(2)}) collective-permute-start(bf16[52,10]{1,0:T(8,128)(2,1)S(1)} %get-tuple-element.347), channel_id=1, source_target_pairs={{16,0},{32,16},{48,32},{64,48},{80,64},{96,80},{112,96},{128,112},... | collective-permute-start | bytes 3128 | tf_op jit(solution)/shard_map/ppermute | solution.py:21
  98.5 17.6 %collective-permute-start.4 = (bf16[52,10]{1,0:T(8,128)(2,1)S(1)}, bf16[52,10]{1,0:T(8,128)(2,1)S(1)}, u32[]{:S(2)}, u32[]{:S(2)}) collective-permute-start(bf16[52,10]{1,0:T(8,128)(2,1)S(1)} %get-tuple-element.346), channel_id=1, source_target_pairs={{0,16},{16,32},{32,48},{48,64},{64,80},{80,96},{96,112},{112,128},... | collective-permute-start | bytes 3128 | tf_op jit(solution)/shard_map/ppermute | solution.py:20
  100.5 15.7 %collective-permute-start.3 = (bf16[52,10]{1,0:T(8,128)(2,1)S(1)}, bf16[52,10]{1,0:T(8,128)(2,1)S(1)}, u32[]{:S(2)}, u32[]{:S(2)}) collective-permute-start(bf16[52,10]{1,0:T(8,128)(2,1)S(1)} %get-tuple-element.345), channel_id=1, source_target_pairs={{16,0},{32,16},{48,32},{64,48},{80,64},{96,80},{112,96},{128,112},... | collective-permute-start | bytes 3128 | tf_op jit(solution)/shard_map/ppermute | solution.py:21
  106.3 9.8 %collective-permute-start.2 = (bf16[52,10]{1,0:T(8,128)(2,1)S(1)}, bf16[52,10]{1,0:T(8,128)(2,1)S(1)}, u32[]{:S(2)}, u32[]{:S(2)}) collective-permute-start(bf16[52,10]{1,0:T(8,128)(2,1)S(1)} %get-tuple-element.344), channel_id=1, source_target_pairs={{0,16},{16,32},{32,48},{48,64},{64,80},{80,96},{96,112},{112,128},... | collective-permute-start | bytes 3128 | tf_op jit(solution)/shard_map/ppermute | solution.py:20
  108.2 8.0 %collective-permute-start.1 = (bf16[52,10]{1,0:T(8,128)(2,1)S(1)}, bf16[52,10]{1,0:T(8,128)(2,1)S(1)}, u32[]{:S(2)}, u32[]{:S(2)}) collective-permute-start(bf16[52,10]{1,0:T(8,128)(2,1)S(1)} %get-tuple-element.340), channel_id=1, source_target_pairs={{16,0},{32,16},{48,32},{64,48},{80,64},{96,80},{112,96},{128,112},... | collective-permute-start | bytes 3128 | tf_op jit(solution)/shard_map/ppermute | solution.py:21
  114.1 7.1 %collective-permute-start = (bf16[52,10]{1,0:T(8,128)(2,1)S(1)}, bf16[52,10]{1,0:T(8,128)(2,1)S(1)}, u32[]{:S(2)}, u32[]{:S(2)}) collective-permute-start(bf16[52,10]{1,0:T(8,128)(2,1)S(1)} %get-tuple-element.339), channel_id=1, source_target_pairs={{0,16},{16,32},{32,48},{48,64},{64,80},{80,96},{96,112},{112,128},... | collective-permute-start | bytes 3128 | tf_op jit(solution)/shard_map/ppermute | solution.py:20
  313.9 49.8 %copy-start.2 = (f32[32,384]{1,0:T(8,128)}, f32[32,384]{1,0:T(8,128)S(1)}, u32[]{:S(2)}) copy-start(f32[32,384]{1,0:T(8,128)S(1)} %add_divide_fusion) | copy-start | bytes 147460
  314.0 5.0 %collective-permute-start.9 = (f32[32,10]{1,0:T(8,128)S(1)}, f32[32,10]{1,0:T(8,128)S(1)}, u32[]{:S(2)}, u32[]{:S(2)}) collective-permute-start(f32[32,10]{1,0:T(8,128)S(1)} %get-tuple-element.338), channel_id=1, source_target_pairs={{16,0},{32,16},{48,32},{64,48},{80,64},{96,80},{112,96},{128,112},... | collective-permute-start | bytes 3848 | tf_op jit(solution)/shard_map/ppermute | solution.py:21
  315.9 7.2 %collective-permute-start.8 = (f32[32,10]{1,0:T(8,128)S(1)}, f32[32,10]{1,0:T(8,128)S(1)}, u32[]{:S(2)}, u32[]{:S(2)}) collective-permute-start(f32[32,10]{1,0:T(8,128)S(1)} %get-tuple-element.337), channel_id=1, source_target_pairs={{0,16},{16,32},{32,48},{48,64},{64,80},{80,96},{96,112},{112,128},... | collective-permute-start | bytes 3848 | tf_op jit(solution)/shard_map/ppermute | solution.py:20
  336.4 5.9 %collective-permute-start.11 = (f32[10,384]{1,0:T(8,128)S(1)}, f32[10,384]{1,0:T(8,128)S(1)}, u32[]{:S(2)}, u32[]{:S(2)}) collective-permute-start(f32[10,384]{1,0:T(8,128)S(1)} %get-tuple-element.336), channel_id=1, source_target_pairs={{1,0},{2,1},{3,2},{4,3},{5,4},{6,5},{7,6},{8,7},{9,8},{10,9},{11,1... | collective-permute-start | bytes 46088 | tf_op jit(solution)/shard_map/ppermute | solution.py:21
  338.3 11.7 %collective-permute-start.10 = (f32[10,384]{1,0:T(8,128)S(1)}, f32[10,384]{1,0:T(8,128)S(1)}, u32[]{:S(2)}, u32[]{:S(2)}) collective-permute-start(f32[10,384]{1,0:T(8,128)S(1)} %get-tuple-element.335), channel_id=1, source_target_pairs={{0,1},{1,2},{2,3},{3,4},{4,5},{5,6},{6,7},{7,8},{8,9},{9,10},{10,1... | collective-permute-start | bytes 46088 | tf_op jit(solution)/shard_map/ppermute | solution.py:20
